TPU v7x, 256 devices: a whole 4x4x8 slice. The times are simulated.
256 devices in a mesh: shard: 32 (over z, y), dp: 8 (over x, core).
Axes of the slice: x: 4, y: 4, z: 8, core: 2. Of those that a mesh axis runs over, the one named last changes fastest.
Arguments:
- cold_table: bfloat16 [65536, 256], P('shard'), may hold values from -6 to 6
- cold_accum: float32 [65536], P('shard'), may hold values from 0.005 to 0.5
- dither_bits: int32 [65536, 256], P('shard'), may hold values from 0 to 65280
- hot_table: float32 [1024, 256], replicated, may hold values from -6 to 6
- hot_accum: float32 [1024], replicated, may hold values from 1 to 100
- w_flat: bfloat16 [4096, 512], replicated, may hold values from -0.09375 to 0.09375
- w_inter: bfloat16 [256, 512], replicated, may hold values from -0.09375 to 0.09375
- hidden_bias: float32 [512], replicated, may hold values from -1 to 1
- w_out: float32 [512], replicated, may hold values from -0.25 to 0.25
- targets: float32 [131072], P(('shard', 'dp')), may hold values from 0 to 1
- hot_ids: int32 [131072, 8], P(('shard', 'dp')), may hold values from 0 to 1023
- cold_slots: int32 [131072, 8], P(('shard', 'dp')), may hold values from 0 to 2047, as said below
- requests: int32 [16384, 64], P(('shard', 'dp')), may hold values from 0 to 2047, as said below
- counts: int32 [512, 32], P(('shard', 'dp')), may hold values from 1 to 64, as said below
Outputs:
- cold_out: bfloat16 [65536, 256], P('shard')
- cold_accum_out: float32 [65536], P('shard')
- hot_out: float32 [1024, 256], replicated
- hot_accum_out: float32 [1024], replicated
Inputs may be any that keep to these rules, and one draw needn't show every extreme that they name: `requests`: in each row of 64 entries (one device, micro-batch and shard) the entries name distinct rows of that shard's 2048; only the first counts-many are live, the rest name arbitrary rows. `counts`: in every draw, each device has in each micro-batch a shard with exactly 64 live slots. `cold_slots`: index into its device's request rows of that micro-batch, shard * 64 + slot; always a live slot, and every live slot is named by some lookup.
All inputs are finite; a program needn't handle non-finite values.
Results may differ from a plain program's by a relative error of at most 0.001.
The roundings to bfloat16 on the way count: a program that leaves them out, or rounds other values in their place, can miss the bound.
Values may be sent and summed in bfloat16 or wider, within the bound.
No kernel may reach another device: no remote copies, remote signals or barrier semaphores. Data moves between devices by JAX's collectives and lax.ppermute only.
A program may use at most 128 MiB of HBM per device.

v0:
```python
import jax
import jax.numpy as jnp
from jax import lax
from jax.sharding import PartitionSpec as P

MB = 2
BATCH = 256
learn_rate = 0.3


def backprop(stacked, targets, w_flat, w_inter, hidden_bias, w_out):
    row_count, feature_count, row_width = stacked.shape
    flattened = stacked.reshape(row_count, feature_count * row_width)
    pair_dots = (
        jnp.einsum("sfe,sge->sfg", stacked, stacked, preferred_element_type=jnp.float32)
        * row_width ** (-0.5)
    ).astype(jnp.bfloat16)
    pre_act = jnp.dot(flattened, w_flat, preferred_element_type=jnp.float32)
    pre_act = pre_act + jnp.dot(
        pair_dots.reshape(row_count, feature_count * feature_count),
        w_inter,
        preferred_element_type=jnp.float32,
    )
    pre_act = pre_act + hidden_bias
    gated = jax.nn.sigmoid(pre_act)
    logits = jnp.sum(pre_act * gated * w_out, axis=-1)
    residual = jax.nn.sigmoid(logits) - targets
    slopes = (residual[:, None] * w_out * gated * (1.0 + pre_act * (1.0 - gated))).astype(
        jnp.bfloat16
    )
    back_flat = jnp.dot(slopes, w_flat.T, preferred_element_type=jnp.float32)
    back_pairs = jnp.dot(slopes, w_inter.T, preferred_element_type=jnp.float32).reshape(
        row_count, feature_count, feature_count
    )
    mirror = ((back_pairs + jnp.swapaxes(back_pairs, 1, 2)) * row_width ** (-0.5)).astype(
        jnp.bfloat16
    )
    return back_flat.reshape(row_count, feature_count, row_width) + jnp.einsum(
        "sfg,sge->sfe", mirror, stacked, preferred_element_type=jnp.float32
    )


def adagrad_rows(table_rows, accum, gradient):
    accum_new = accum + jnp.mean(gradient * gradient, axis=-1)
    updated = table_rows - learn_rate * gradient / jnp.sqrt(accum_new)[:, None]
    return (updated, accum_new)


def requantize(updated, bits, touched):
    grid_step = jnp.max(jnp.abs(updated), axis=-1, keepdims=True) / 8.0
    dither = bits.astype(jnp.float32) * (1.0 / 65280.0) - 0.5
    return jnp.where(touched[:, None], updated + grid_step * dither, updated).astype(jnp.bfloat16)


def on_device(
    cold_table,
    cold_accum,
    dither_bits,
    hot_table,
    hot_accum,
    w_flat,
    w_inter,
    hidden_bias,
    w_out,
    targets,
    hot_ids,
    cold_slots,
    requests,
    counts,
):
    shards = lax.axis_size("shard")
    capacity = requests.shape[1]
    row_count = cold_table.shape[0]
    row_width = cold_table.shape[1]
    hot_count = hot_table.shape[0]
    cold_feats = cold_slots.shape[1]
    hot_grad = jnp.zeros((hot_count, row_width), jnp.float32)
    cold_grad = jnp.zeros((row_count, row_width), jnp.float32)
    touched = jnp.zeros((row_count,), jnp.float32)
    for micro_index in range(MB):
        asked_rows = requests[micro_index * shards : (micro_index + 1) * shards]
        requested = lax.all_to_all(asked_rows, "shard", split_axis=0, concat_axis=0, tiled=True)
        fetched_rows = lax.all_to_all(
            cold_table[requested], "shard", split_axis=0, concat_axis=0, tiled=True
        )
        first = micro_index * BATCH
        slot_part = cold_slots[first : first + BATCH]
        hot_part = hot_ids[first : first + BATCH]
        cold_vectors = fetched_rows.reshape(shards * capacity, row_width)[slot_part]
        stacked = jnp.concatenate([cold_vectors, hot_table[hot_part].astype(jnp.bfloat16)], axis=1)
        gradients = backprop(
            stacked, targets[first : first + BATCH], w_flat, w_inter, hidden_bias, w_out
        )
        slot_grad = jax.ops.segment_sum(
            gradients[:, :cold_feats].reshape(-1, row_width),
            slot_part.reshape(-1),
            num_segments=shards * capacity,
        )
        hot_term = jax.ops.segment_sum(
            gradients[:, cold_feats:].reshape(-1, row_width),
            hot_part.reshape(-1),
            num_segments=hot_count,
        )
        slot_grad, hot_term = (slot_grad.reshape(shards, capacity, row_width), hot_term)
        hot_grad = hot_grad + hot_term
        owner_grad, count_in = (
            lax.all_to_all(
                slot_grad.astype(jnp.bfloat16), "shard", split_axis=0, concat_axis=0, tiled=True
            ).astype(slot_grad.dtype),
            lax.all_to_all(counts[micro_index], "shard", split_axis=0, concat_axis=0, tiled=True),
        )
        cold_grad = cold_grad + jax.ops.segment_sum(
            owner_grad.reshape(-1, row_width), requested.reshape(-1), num_segments=row_count
        )
        live_mask = (jnp.arange(capacity, dtype=jnp.int32)[None, :] < count_in[:, None]).astype(
            jnp.float32
        )
        touched = touched + jax.ops.segment_sum(
            live_mask.reshape(-1), requested.reshape(-1), num_segments=row_count
        )
    summed_grad, summed_hits = (
        lax.psum(cold_grad.astype(jnp.bfloat16), "dp").astype(jnp.float32),
        lax.psum(touched.astype(jnp.bfloat16), "dp").astype(jnp.float32),
    )
    averaged = summed_grad / jnp.maximum(summed_hits, 1.0)[:, None]
    updated, cold_accum_out = adagrad_rows(cold_table.astype(jnp.float32), cold_accum, averaged)
    cold_out = requantize(updated, dither_bits, summed_hits > 0.5)
    total_hot = lax.psum(hot_grad, ("shard", "dp"))
    hot_out, hot_accum_out = adagrad_rows(hot_table, hot_accum, total_hot)
    return (cold_out, cold_accum_out, hot_out, hot_accum_out)


def solution(mesh):
    return jax.shard_map(
        on_device,
        mesh=mesh,
        in_specs=(
            P("shard", None),
            P("shard"),
            P("shard", None),
            P(),
            P(),
            P(),
            P(),
            P(),
            P(),
            P(("shard", "dp")),
            P(("shard", "dp"), None),
            P(("shard", "dp"), None),
            P(("shard", "dp"), None),
            P(("shard", "dp"), None),
        ),
        out_specs=(P("shard", None), P("shard"), P(), P()),
        check_vma=False,
    )
```

profile of v0, /device:TPU:8, one launch (start us, length us, event | category | flops | bytes accessed | tf_op | source)
XLA Modules:
  0.0 695.9 jit_solution(9611974366071185003)
XLA Ops:
  9.4 20.0 %all_to_all.62 = s32[32,1,64]{2,1,0:T(1,128)S(1)} all-to-all(s32[32,1,64]{2,1,0:T(1,128)S(1)} %bitcast.113), channel_id=1, replica_groups=mesh['shard'=32,'dp'=8] {'shard'}, dimensions={0} | all-to-all | bytes 16384 | tf_op jit(solution)/shard_map/all_to_all | solution.py:82
  29.4 4.9 all-to-all-start
  34.5 9.9 %gather_fusion.3 = bf16[2048,256]{1,0:T(8,128)(2,1)} fusion(bf16[2048,256]{1,0:T(8,128)(2,1)} %param.14, s32[2048]{0:T(1024)S(1)} %broadcast_clamp_fusion.3), kind=kCustom, calls=%fused_computation.3 | custom fusion | bytes 2105344 | tf_op jit(solution)/shard_map/gather | solution.py:84
  44.3 10.0 %all-to-all-start.6 = ((bf16[32,64,256]{2,1,0:T(8,128)(2,1)}), bf16[32,64,256]{2,1,0:T(8,128)(2,1)S(1)}, u32[]{:S(2)}, u32[]{:S(2)}) async-start(bf16[32,64,256]{2,1,0:T(8,128)(2,1)} %bitcast.16), calls=%async_computation.6 | async-start | bytes 2097152 | tf_op jit(solution)/shard_map/all_to_all | solution.py:83
  54.5 9.1 %gather_fusion = bf16[2048,256]{1,0:T(8,128)(2,1)} fusion(bf16[2048,256]{1,0:T(8,128)(2,1)S(1)} %copy-done.2, s32[2048]{0:T(1024)S(1)} %broadcast_clamp_fusion.5), kind=kCustom, calls=%fused_computation | custom fusion | bytes 2105344 | tf_op jit(solution)/shard_map/gather | solution.py:84
  63.5 17.2 %all-to-all-done.6 = bf16[32,64,256]{2,1,0:T(8,128)(2,1)S(1)} async-done(((bf16[32,64,256]{2,1,0:T(8,128)(2,1)}), bf16[32,64,256]{2,1,0:T(8,128)(2,1)S(1)}, u32[]{:S(2)}, u32[]{:S(2)}) %all-to-all-start.6) | async-done | bytes 1048608 | tf_op jit(solution)/shard_map/all_to_all | solution.py:83
  80.7 5.6 all-to-all-start.4
  98.1 8.4 %gather_fusion.5 = bf16[2048,256]{1,0:T(8,128)(2,1)} fusion(f32[1024,256]{1,0:T(8,128)S(1)} %copy-done.1, s32[2048]{0:T(1024)S(1)} %broadcast_clamp_fusion), kind=kCustom, calls=%fused_computation.5 | custom fusion | bytes 2105344 | tf_op jit(solution)/shard_map/gather | solution.py:90
  106.5 8.5 %gather_fusion.2 = bf16[2048,256]{1,0:T(8,128)(2,1)} fusion(f32[1024,256]{1,0:T(8,128)S(1)} %copy-done.1, s32[2048]{0:T(1024)S(1)} %broadcast_clamp_fusion.1), kind=kCustom, calls=%fused_computation.2 | custom fusion | bytes 2105344 | tf_op jit(solution)/shard_map/gather | solution.py:90
  115.0 9.0 %gather_fusion.4 = bf16[2048,256]{1,0:T(8,128)(2,1)} fusion(bf16[2048,256]{1,0:T(8,128)(2,1)S(1)} %bitcast.86, s32[2048]{0:T(1024)S(1)} %broadcast_clamp_fusion.2), kind=kCustom, calls=%fused_computation.4 | custom fusion | bytes 2105344 | tf_op jit(solution)/shard_map/gather | solution.py:89
  124.1 4.4 fusion.27
  129.9 10.5 %all-to-all-start.3 = ((s32[32,1,1]{2,1,0:T(1,128)}), s32[32,1,1]{2,1,0:T(1,128)}, u32[]{:S(2)}, u32[]{:S(2)}) async-start(s32[32,1,1]{2,1,0:T(1,128)} %copy.67), calls=%async_computation.3 | async-start | bytes 32768 | tf_op jit(solution)/shard_map/all_to_all | solution.py:110
  140.5 9.9 %gather_fusion.1 = bf16[2048,256]{1,0:T(8,128)(2,1)} fusion(bf16[2048,256]{1,0:T(8,128)(2,1)} %bitcast.6, s32[2048]{0:T(1024)S(1)} %broadcast_clamp_fusion.4), kind=kCustom, calls=%fused_computation.1 | custom fusion | bytes 2105344 | tf_op jit(solution)/shard_map/gather | solution.py:89
  150.3 4.3 fusion.28
  154.7 1.5 pad_maximum_fusion
  156.2 3.2 copy.77
  160.4 3.9 copy.84
  164.2 3.2 copy.71
  168.4 2.7 copy.82
  171.2 2.8 fusion.37
  177.6 3.2 fusion.35
  181.0 1.9 copy.73
  182.8 5.9 copy.83
  188.7 10.1 %all-to-all-start.1 = ((s32[32,1,1]{2,1,0:T(1,128)}), s32[32,1,1]{2,1,0:T(1,128)S(1)}, u32[]{:S(2)}, u32[]{:S(2)}) async-start(s32[32,1,1]{2,1,0:T(1,128)} %copy.66), calls=%async_computation.1 | async-start | bytes 32768 | tf_op jit(solution)/shard_map/all_to_all | solution.py:110
  198.8 5.8 bitcast_add_fusion.1
  204.6 13.5 %scatter_custom_fusion.2 = f32[2048,256]{1,0:T(8,128)} fusion(s32[2048]{0:T(1024)} %reshape.252, f32[256,16,256]{2,1,0:T(8,128)} %bitcast_add_fusion.1, f32[]{:T(128)} %constant.13.clone.1), kind=kCustom, calls=%fused_computation.25 | custom fusion | flops 524288 | bytes 4194816 | tf_op jit(solution)/shard_map/scatter-add | solution.py:94
  218.1 2.7 convert_element_type.84
  220.8 9.8 %all-to-all-start.5 = ((bf16[32,64,256]{2,1,0:T(8,128)(2,1)}), bf16[32,64,256]{2,1,0:T(8,128)(2,1)}, u32[]{:S(2)}, u32[]{:S(2)}) async-start(bf16[32,64,256]{2,1,0:T(8,128)(2,1)} %bitcast.104), calls=%async_computation.5 | async-start | bytes 2097152 | tf_op jit(solution)/shard_map/all_to_all | solution.py:107
  233.5 1.9 copy.79
  235.4 3.6 fusion.38
  239.0 1.8 copy.85
  240.8 2.9 bitcast_add_fusion
  243.7 13.6 %scatter_custom_fusion.4 = f32[2048,256]{1,0:T(8,128)} fusion(s32[2048]{0:T(1024)} %reshape.268, f32[256,16,256]{2,1,0:T(8,128)} %bitcast_add_fusion, f32[]{:T(128)} %constant.13.clone.1), kind=kCustom, calls=%fused_computation.23 | custom fusion | flops 524288 | bytes 4194816 | tf_op jit(solution)/shard_map/scatter-add | solution.py:94
  257.3 2.7 convert_element_type.90
  260.0 10.0 %all-to-all-start.7 = ((bf16[32,64,256]{2,1,0:T(8,128)(2,1)}), bf16[32,64,256]{2,1,0:T(8,128)(2,1)}, u32[]{:S(2)}, u32[]{:S(2)}) async-start(bf16[32,64,256]{2,1,0:T(8,128)(2,1)} %bitcast.24), calls=%async_computation.7 | async-start | bytes 2097152 | tf_op jit(solution)/shard_map/all_to_all | solution.py:107
  275.1 11.3 %scatter_custom_fusion.1 = f32[2048]{0:T(1024)S(1)} fusion(s32[2048]{0:T(1024)S(1)} %reshape.244, f32[2048]{0:T(1024)S(1)} %reshape.246, f32[]{:T(128)} %constant.13.clone.1), kind=kCustom, calls=%fused_computation.87 | custom fusion | flops 2048 | bytes 8196 | tf_op jit(solution)/shard_map/scatter-add | solution.py:118
  286.4 11.3 %scatter_custom_fusion = f32[2048]{0:T(1024)S(1)} fusion(s32[2048]{0:T(1024)S(1)} %reshape.236, f32[2048]{0:T(1024)S(1)} %reshape.238, f32[]{:T(128)} %constant.13.clone.1), kind=kCustom, calls=%fused_computation.89 | custom fusion | flops 2048 | bytes 8196 | tf_op jit(solution)/shard_map/scatter-add | solution.py:118
  297.7 12.4 %scatter_custom_fusion.6 = f32[1024,256]{1,0:T(8,128)S(1)} fusion(s32[2048]{0:T(1024)S(1)} %reshape.284, f32[256,16,256]{2,1,0:T(8,128)} %bitcast_add_fusion.1, f32[]{:T(128)} %constant.13.clone.1), kind=kCustom, calls=%fused_computation.21 | custom fusion | flops 524288 | bytes 3146240 | tf_op jit(solution)/shard_map/scatter-add | solution.py:99
  310.1 13.1 %scatter_custom_fusion.7 = f32[1024,256]{1,0:T(8,128)} fusion(s32[2048]{0:T(1024)S(1)} %reshape.292, f32[256,16,256]{2,1,0:T(8,128)} %bitcast_add_fusion, f32[]{:T(128)} %constant.13.clone.1), kind=kCustom, calls=%fused_computation.19 | custom fusion | flops 524288 | bytes 3146240 | tf_op jit(solution)/shard_map/scatter-add | solution.py:99
  323.2 2.3 add.148
  325.6 12.4 %psum.21 = bf16[2048]{0:T(1024)(128)(2,1)S(1)} all-reduce(bf16[2048]{0:T(1024)(128)(2,1)S(1)} %add_convert_fusion.1), channel_id=1, replica_groups=mesh['shard'=32,'dp'=8] {'dp'}, use_global_device_ids=true, to_apply=%region_2.0 | all-reduce | flops 2048 | bytes 8192 | tf_op jit(solution)/shard_map/psum | solution.py:123
  338.1 247.5 %all-reduce.5.cloned.1.call-done = f32[1024,256]{1,0:T(8,128)} async-done(((f32[1024,256]{1,0:T(8,128)}), f32[1024,256]{1,0:T(8,128)}) %all-reduce.5.cloned.1.call-update) | async-done | bytes 1048592 | tf_op jit(solution)/shard_map/psum | solution.py:128
  587.0 12.6 %scatter_custom_fusion.3 = f32[2048,256]{1,0:T(8,128)} fusion(s32[2048]{0:T(1024)S(1)} %reshape.236, bf16[2048,256]{1,0:T(8,128)(2,1)} %bitcast.28, f32[]{:T(128)} %constant.13.clone.1), kind=kCustom, calls=%fused_computation.30 | custom fusion | flops 1048576 | bytes 3145732 | tf_op jit(solution)/shard_map/scatter-add | solution.py:112
  599.6 12.3 %scatter_custom_fusion.5 = f32[2048,256]{1,0:T(8,128)} fusion(s32[2048]{0:T(1024)S(1)} %reshape.244, bf16[2048,256]{1,0:T(8,128)(2,1)} %bitcast.29, f32[]{:T(128)} %constant.13.clone.1), kind=kCustom, calls=%fused_computation.28 | custom fusion | flops 1048576 | bytes 3145732 | tf_op jit(solution)/shard_map/scatter-add | solution.py:112
  611.9 3.5 add_convert_fusion
  617.3 64.7 %all-reduce.3.cloned.1.call-done = bf16[2048,256]{1,0:T(8,128)(2,1)} async-done(((bf16[2048,256]{1,0:T(8,128)(2,1)}), bf16[2048,256]{1,0:T(8,128)(2,1)}) %all-reduce.3.cloned.1.call-update) | async-done | bytes 1048592 | tf_op jit(solution)/shard_map/psum | solution.py:122
  681.9 1.9 multiply_reduce_fusion
  684.5 2.2 abs_reduce_fusion
  (130 shorter events, 33.9 us)
Async XLA Ops:
  8.0 167.3 %copy-start = (bf16[256,512]{1,0:T(8,128)(2,1)S(1)}, bf16[256,512]{1,0:T(8,128)(2,1)}, u32[]{:S(2)}) copy-start(bf16[256,512]{1,0:T(8,128)(2,1)} %param.20) | copy-start | bytes 786436
  29.4 14.9 %copy-start.12 = (s32[32,1,64]{2,1,0:T(1,128)}, s32[32,1,64]{2,1,0:T(1,128)S(1)}, u32[]{:S(2)}) copy-start(s32[32,1,64]{2,1,0:T(1,128)S(1)} %all_to_all.62) | copy-start | bytes 24580
  29.4 14.9 %all-to-all-start = ((s32[32,1,64]{2,1,0:T(1,128)}), s32[32,1,64]{2,1,0:T(1,128)S(1)}, u32[]{:S(2)}, u32[]{:S(2)}) async-start(s32[32,1,64]{2,1,0:T(1,128)} %bitcast), calls=%async_computation | async-start | bytes 32768 | tf_op jit(solution)/shard_map/all_to_all | solution.py:82
  44.3 10.1 %copy-start.2 = (bf16[2048,256]{1,0:T(8,128)(2,1)S(1)}, bf16[2048,256]{1,0:T(8,128)(2,1)}, u32[]{:S(2)}) copy-start(bf16[2048,256]{1,0:T(8,128)(2,1)} %param.14) | copy-start | bytes 3145732
  44.3 36.4 %all-to-all-start.6 = ((bf16[32,64,256]{2,1,0:T(8,128)(2,1)}), bf16[32,64,256]{2,1,0:T(8,128)(2,1)S(1)}, u32[]{:S(2)}, u32[]{:S(2)}) async-start(bf16[32,64,256]{2,1,0:T(8,128)(2,1)} %bitcast.16), calls=%async_computation.6 | async-start | bytes 2097152 | tf_op jit(solution)/shard_map/all_to_all | solution.py:83
  63.5 22.8 %copy-start.27 = (s32[2,32]{1,0:T(2,128)S(1)}, s32[2,32]{1,0:T(2,128)}, u32[]{:S(2)}) copy-start(s32[2,32]{1,0:T(2,128)} %param.27) | copy-start | bytes 772
  63.5 24.2 %copy-start.21 = (s32[512,8]{0,1:T(8,128)S(1)}, s32[512,8]{0,1:T(8,128)}, u32[]{:S(2)}) copy-start(s32[512,8]{0,1:T(8,128)} %param.25) | copy-start | bytes 49156
  63.5 34.5 %copy-start.1 = (f32[1024,256]{1,0:T(8,128)S(1)}, f32[1024,256]{1,0:T(8,128)}, u32[]{:S(2)}) copy-start(f32[1024,256]{1,0:T(8,128)} %param.17) | copy-start | bytes 3145732
  80.7 49.2 %all-to-all-start.4 = ((bf16[32,64,256]{2,1,0:T(8,128)(2,1)}), bf16[32,64,256]{2,1,0:T(8,128)(2,1)}, u32[]{:S(2)}, u32[]{:S(2)}) async-start(bf16[32,64,256]{2,1,0:T(8,128)(2,1)} %bitcast.103), calls=%async_computation.4 | async-start | bytes 2097152 | tf_op jit(solution)/shard_map/all_to_all | solution.py:83
  98.1 8.4 %copy-start.18 = (s32[2048]{0:T(1024)S(1)}, s32[2048]{0:T(1024)}, u32[]{:S(2)}) copy-start(s32[2048]{0:T(1024)} %reshape.204) | copy-start | bytes 24580
  106.5 8.5 %copy-start.16 = (s32[2048]{0:T(1024)S(1)}, s32[2048]{0:T(1024)}, u32[]{:S(2)}) copy-start(s32[2048]{0:T(1024)} %reshape.196) | copy-start | bytes 24580
  106.5 8.5 %copy-start.17 = (s32[2048]{0:T(1024)S(1)}, s32[2048]{0:T(1024)}, u32[]{:S(2)}) copy-start(s32[2048]{0:T(1024)} %reshape.220) | copy-start | bytes 24580
  124.0 4.4 copy-start.4
  124.0 4.4 copy-start.5
  129.9 58.8 %all-to-all-start.3 = ((s32[32,1,1]{2,1,0:T(1,128)}), s32[32,1,1]{2,1,0:T(1,128)}, u32[]{:S(2)}, u32[]{:S(2)}) async-start(s32[32,1,1]{2,1,0:T(1,128)} %copy.67), calls=%async_computation.3 | async-start | bytes 32768 | tf_op jit(solution)/shard_map/all_to_all | solution.py:110
  150.3 4.3 copy-start.7
  150.3 4.3 copy-start.8
  168.4 2.8 copy-start.3
  174.1 1.3 copy-start.24
  174.1 1.5 copy-start.25
  175.6 0.7 copy-start.26
  188.7 32.0 %all-to-all-start.1 = ((s32[32,1,1]{2,1,0:T(1,128)}), s32[32,1,1]{2,1,0:T(1,128)S(1)}, u32[]{:S(2)}, u32[]{:S(2)}) async-start(s32[32,1,1]{2,1,0:T(1,128)} %copy.66), calls=%async_computation.1 | async-start | bytes 32768 | tf_op jit(solution)/shard_map/all_to_all | solution.py:110
  220.8 9.8 %copy-start.14 = (s32[32,1,1]{2,1,0:T(1,128)}, s32[32,1,1]{2,1,0:T(1,128)S(1)}, u32[]{:S(2)}) copy-start(s32[32,1,1]{2,1,0:T(1,128)S(1)} %all-to-all-done.1) | copy-start | bytes 388
  220.8 39.2 %all-to-all-start.5 = ((bf16[32,64,256]{2,1,0:T(8,128)(2,1)}), bf16[32,64,256]{2,1,0:T(8,128)(2,1)}, u32[]{:S(2)}, u32[]{:S(2)}) async-start(bf16[32,64,256]{2,1,0:T(8,128)(2,1)} %bitcast.104), calls=%async_computation.5 | async-start | bytes 2097152 | tf_op jit(solution)/shard_map/all_to_all | solution.py:107
  239.0 1.8 copy-start.6
  239.0 1.8 copy-start.10
  257.3 12.9 %copy-start.20 = (s32[256,8]{0,1:T(8,128)S(1)}, s32[256,8]{0,1:T(8,128)}, u32[]{:S(2)}) copy-start(s32[256,8]{0,1:T(8,128)} %get-tuple-element.14) | copy-start | bytes 24580
  257.3 13.2 %copy-start.19 = (s32[256,8]{0,1:T(8,128)S(1)}, s32[256,8]{0,1:T(8,128)}, u32[]{:S(2)}) copy-start(s32[256,8]{0,1:T(8,128)} %get-tuple-element.17) | copy-start | bytes 24580
  260.0 12.3 %copy-start.15 = (s32[32,1,1]{2,1,0:T(1,128)S(1)}, s32[32,1,1]{2,1,0:T(1,128)}, u32[]{:S(2)}) copy-start(s32[32,1,1]{2,1,0:T(1,128)} %copy-done.14) | copy-start | bytes 388
  260.0 13.6 %copy-start.13 = (s32[32,1,64]{2,1,0:T(1,128)S(1)}, s32[32,1,64]{2,1,0:T(1,128)}, u32[]{:S(2)}) copy-start(s32[32,1,64]{2,1,0:T(1,128)} %copy-done.12) | copy-start | bytes 24580
  260.0 339.7 %all-to-all-start.7 = ((bf16[32,64,256]{2,1,0:T(8,128)(2,1)}), bf16[32,64,256]{2,1,0:T(8,128)(2,1)}, u32[]{:S(2)}, u32[]{:S(2)}) async-start(bf16[32,64,256]{2,1,0:T(8,128)(2,1)} %bitcast.24), calls=%async_computation.7 | async-start | bytes 2097152 | tf_op jit(solution)/shard_map/all_to_all | solution.py:107
  269.9 315.6 %all-reduce.5.cloned.1.call-start = ((), (), s32[]{:S(2)}) async-start(), calls=%async_computation.9 | async-start | bytes 2097152 | tf_op jit(solution)/shard_map/psum | solution.py:128
  325.5 356.4 %all-reduce.3.cloned.1.call-start = ((), (), s32[]{:S(2)}) async-start(), calls=%async_computation.8 | async-start | bytes 2097152 | tf_op jit(solution)/shard_map/psum | solution.py:122
  611.9 3.5 copy-start.23
  611.9 4.1 copy-start.9
  616.1 67.8 %copy-start.22 = (f32[2048]{0:T(1024)S(1)}, f32[2048]{0:T(1024)}, u32[]{:S(2)}) copy-start(f32[2048]{0:T(1024)} %param.15) | copy-start | bytes 24580
  684.5 2.2 copy-start.11
Sparse Core Ops, SparseCore 0:
  325.6 259.8 all-reduce.4
Sparse Core Ops, SparseCore 1:
  615.5 66.3 all-reduce.2
where the time goes:
time: 702 us; the launch traced here: 696 us
  waiting for transfers between devices  329 us (47%)
  other arithmetic  133 us (19%)
  local copies, waits for them, and re-layouts  92.7 us (13%)
  starting transfers between devices  61.3 us (9%)
  blocking collectives  32.5 us (5%)
  matrix products  30.5 us (4%)
  between operations  16.3 us (2%)
    psum x1, waiting for transfers between devices, on_device(): total_hot = lax.psum(hot_grad, ('shard', 'dp'))  248 us
    psum x1, waiting for transfers between devices, on_device(): lax.psum(cold_grad.astype(jnp.bfloat16), 'dp').astype(jnp.float32)  64.7 us
    scatter-add x2, other arithmetic, on_device(): jax.ops.segment_sum(gradients[:, :cold_feats].reshape(-1, row_width), slo...  27.1 us
    scatter-add x2, other arithmetic, on_device(): jax.ops.segment_sum(gradients[:, cold_feats:].reshape(-1, row_width), hot...  25.5 us
    scatter-add x2, other arithmetic, on_device(): jax.ops.segment_sum(owner_grad.reshape(-1, row_width), requested.reshape(...  24.9 us
    scatter-add x2, other arithmetic, on_device(): jax.ops.segment_sum(live_mask.reshape(-1), requested.reshape(-1), num_seg...  22.6 us
    all_to_all x2, starting transfers between devices, on_device(): lax.all_to_all(counts[micro_index], 'shard', split_axis=0, concat_axis=0,...  20.6 us
    all_to_all x1, blocking collectives, on_device(): lax.all_to_all(asked_rows, 'shard', split_axis=0, concat_axis=0, tiled=True)  20 us
  transfers between devices with their start and end apart: 9, of which 3 were waited for; matrix products, arithmetic and copies ran while one was open for 33% of the time, Pallas kernels for 0%

commit v1 on v0

--- a/solution.py
+++ b/solution.py
@@ -125,7 +125,7 @@
     averaged = summed_grad / jnp.maximum(summed_hits, 1.0)[:, None]
     updated, cold_accum_out = adagrad_rows(cold_table.astype(jnp.float32), cold_accum, averaged)
     cold_out = requantize(updated, dither_bits, summed_hits > 0.5)
-    total_hot = lax.psum(hot_grad, ("shard", "dp"))
+    total_hot = lax.psum(lax.psum(hot_grad, "shard"), "dp")
     hot_out, hot_accum_out = adagrad_rows(hot_table, hot_accum, total_hot)
     return (cold_out, cold_accum_out, hot_out, hot_accum_out)
 

time: 702 us -> 633 us (0.902)
  waiting for transfers between devices: 329 us -> 262 us
    psum x1 -> x2, waiting for transfers between devices: 248 us -> 179 us  [on_device(): total_hot = lax.psum(lax.psum(hot_grad, 'shard'), 'dp')]
  transfers between devices with their start and end apart: 9 -> 10, of which waited for: 3 -> 4; matrix products, arithmetic and copies ran while one was open for 33% -> 37% of each run, Pallas kernels for 0% -> 0%
where the time goes in v1:
time: 633 us; the launch traced here: 627 us
  waiting for transfers between devices  262 us (41%)
  other arithmetic  133 us (21%)
  local copies, waits for them, and re-layouts  92.7 us (15%)
  starting transfers between devices  61.2 us (10%)
  blocking collectives  32.5 us (5%)
  matrix products  30.5 us (5%)
  between operations  14.6 us (2%)
    psum x2, waiting for transfers between devices, on_device(): total_hot = lax.psum(lax.psum(hot_grad, 'shard'), 'dp')  179 us
    psum x1, waiting for transfers between devices, on_device(): lax.psum(cold_grad.astype(jnp.bfloat16), 'dp').astype(jnp.float32)  65.4 us
    scatter-add x2, other arithmetic, on_device(): jax.ops.segment_sum(gradients[:, :cold_feats].reshape(-1, row_width), slo...  27.1 us
    scatter-add x2, other arithmetic, on_device(): jax.ops.segment_sum(gradients[:, cold_feats:].reshape(-1, row_width), hot...  25.5 us
    scatter-add x2, other arithmetic, on_device(): jax.ops.segment_sum(owner_grad.reshape(-1, row_width), requested.reshape(...  24.9 us
    scatter-add x2, other arithmetic, on_device(): jax.ops.segment_sum(live_mask.reshape(-1), requested.reshape(-1), num_seg...  22.6 us
    all_to_all x2, starting transfers between devices, on_device(): lax.all_to_all(counts[micro_index], 'shard', split_axis=0, concat_axis=0,...  20.6 us
    all_to_all x1, blocking collectives, on_device(): lax.all_to_all(asked_rows, 'shard', split_axis=0, concat_axis=0, tiled=True)  20 us
  transfers between devices with their start and end apart: 10, of which 4 were waited for; matrix products, arithmetic and copies ran while one was open for 37% of the time, Pallas kernels for 0%

profile of v1, /device:TPU:8, one launch (start us, length us, event | category | flops | bytes accessed | tf_op | source)
XLA Modules:
  0.0 626.7 jit_solution(16338508620922170230)
XLA Ops:
  8.6 20.0 %all_to_all.62 = s32[32,1,64]{2,1,0:T(1,128)S(1)} all-to-all(s32[32,1,64]{2,1,0:T(1,128)S(1)} %bitcast.113), channel_id=1, replica_groups=mesh['shard'=32,'dp'=8] {'shard'}, dimensions={0} | all-to-all | bytes 16384 | tf_op jit(solution)/shard_map/all_to_all | solution.py:82
  28.6 4.9 all-to-all-start
  33.6 9.9 %gather_fusion.3 = bf16[2048,256]{1,0:T(8,128)(2,1)} fusion(bf16[2048,256]{1,0:T(8,128)(2,1)} %param.14, s32[2048]{0:T(1024)S(1)} %broadcast_clamp_fusion.3), kind=kCustom, calls=%fused_computation.3 | custom fusion | bytes 2105344 | tf_op jit(solution)/shard_map/gather | solution.py:84
  43.5 10.0 %all-to-all-start.6 = ((bf16[32,64,256]{2,1,0:T(8,128)(2,1)}), bf16[32,64,256]{2,1,0:T(8,128)(2,1)S(1)}, u32[]{:S(2)}, u32[]{:S(2)}) async-start(bf16[32,64,256]{2,1,0:T(8,128)(2,1)} %bitcast.16), calls=%async_computation.6 | async-start | bytes 2097152 | tf_op jit(solution)/shard_map/all_to_all | solution.py:83
  53.6 9.1 %gather_fusion = bf16[2048,256]{1,0:T(8,128)(2,1)} fusion(bf16[2048,256]{1,0:T(8,128)(2,1)S(1)} %copy-done.2, s32[2048]{0:T(1024)S(1)} %broadcast_clamp_fusion.5), kind=kCustom, calls=%fused_computation | custom fusion | bytes 2105344 | tf_op jit(solution)/shard_map/gather | solution.py:84
  62.7 17.2 %all-to-all-done.6 = bf16[32,64,256]{2,1,0:T(8,128)(2,1)S(1)} async-done(((bf16[32,64,256]{2,1,0:T(8,128)(2,1)}), bf16[32,64,256]{2,1,0:T(8,128)(2,1)S(1)}, u32[]{:S(2)}, u32[]{:S(2)}) %all-to-all-start.6) | async-done | bytes 1048608 | tf_op jit(solution)/shard_map/all_to_all | solution.py:83
  79.9 5.6 all-to-all-start.4
  97.2 8.4 %gather_fusion.5 = bf16[2048,256]{1,0:T(8,128)(2,1)} fusion(f32[1024,256]{1,0:T(8,128)S(1)} %copy-done.1, s32[2048]{0:T(1024)S(1)} %broadcast_clamp_fusion), kind=kCustom, calls=%fused_computation.5 | custom fusion | bytes 2105344 | tf_op jit(solution)/shard_map/gather | solution.py:90
  105.7 8.5 %gather_fusion.2 = bf16[2048,256]{1,0:T(8,128)(2,1)} fusion(f32[1024,256]{1,0:T(8,128)S(1)} %copy-done.1, s32[2048]{0:T(1024)S(1)} %broadcast_clamp_fusion.1), kind=kCustom, calls=%fused_computation.2 | custom fusion | bytes 2105344 | tf_op jit(solution)/shard_map/gather | solution.py:90
  114.2 9.0 %gather_fusion.4 = bf16[2048,256]{1,0:T(8,128)(2,1)} fusion(bf16[2048,256]{1,0:T(8,128)(2,1)S(1)} %bitcast.86, s32[2048]{0:T(1024)S(1)} %broadcast_clamp_fusion.2), kind=kCustom, calls=%fused_computation.4 | custom fusion | bytes 2105344 | tf_op jit(solution)/shard_map/gather | solution.py:89
  123.2 4.4 fusion.27
  129.1 10.5 %all-to-all-start.3 = ((s32[32,1,1]{2,1,0:T(1,128)}), s32[32,1,1]{2,1,0:T(1,128)}, u32[]{:S(2)}, u32[]{:S(2)}) async-start(s32[32,1,1]{2,1,0:T(1,128)} %copy.67), calls=%async_computation.3 | async-start | bytes 32768 | tf_op jit(solution)/shard_map/all_to_all | solution.py:110
  139.6 9.9 %gather_fusion.1 = bf16[2048,256]{1,0:T(8,128)(2,1)} fusion(bf16[2048,256]{1,0:T(8,128)(2,1)} %bitcast.6, s32[2048]{0:T(1024)S(1)} %broadcast_clamp_fusion.4), kind=kCustom, calls=%fused_computation.1 | custom fusion | bytes 2105344 | tf_op jit(solution)/shard_map/gather | solution.py:89
  149.5 4.3 fusion.28
  155.4 3.2 copy.77
  159.5 3.9 copy.84
  163.4 3.2 copy.71
  167.6 2.7 copy.82
  170.4 2.8 fusion.37
  176.8 3.2 fusion.35
  180.1 1.9 copy.73
  182.0 5.9 copy.83
  187.9 10.1 %all-to-all-start.1 = ((s32[32,1,1]{2,1,0:T(1,128)}), s32[32,1,1]{2,1,0:T(1,128)S(1)}, u32[]{:S(2)}, u32[]{:S(2)}) async-start(s32[32,1,1]{2,1,0:T(1,128)} %copy.66), calls=%async_computation.1 | async-start | bytes 32768 | tf_op jit(solution)/shard_map/all_to_all | solution.py:110
  198.0 5.8 bitcast_add_fusion.1
  203.7 13.5 %scatter_custom_fusion.2 = f32[2048,256]{1,0:T(8,128)} fusion(s32[2048]{0:T(1024)} %reshape.252, f32[256,16,256]{2,1,0:T(8,128)} %bitcast_add_fusion.1, f32[]{:T(128)} %constant.13.clone.1), kind=kCustom, calls=%fused_computation.25 | custom fusion | flops 524288 | bytes 4194816 | tf_op jit(solution)/shard_map/scatter-add | solution.py:94
  217.2 2.7 convert_element_type.84
  219.9 9.8 %all-to-all-start.5 = ((bf16[32,64,256]{2,1,0:T(8,128)(2,1)}), bf16[32,64,256]{2,1,0:T(8,128)(2,1)}, u32[]{:S(2)}, u32[]{:S(2)}) async-start(bf16[32,64,256]{2,1,0:T(8,128)(2,1)} %bitcast.104), calls=%async_computation.5 | async-start | bytes 2097152 | tf_op jit(solution)/shard_map/all_to_all | solution.py:107
  232.7 1.9 copy.79
  234.5 3.6 fusion.38
  238.1 1.8 copy.85
  239.9 2.9 bitcast_add_fusion
  242.8 13.6 %scatter_custom_fusion.4 = f32[2048,256]{1,0:T(8,128)} fusion(s32[2048]{0:T(1024)} %reshape.268, f32[256,16,256]{2,1,0:T(8,128)} %bitcast_add_fusion, f32[]{:T(128)} %constant.13.clone.1), kind=kCustom, calls=%fused_computation.23 | custom fusion | flops 524288 | bytes 4194816 | tf_op jit(solution)/shard_map/scatter-add | solution.py:94
  256.4 2.7 convert_element_type.90
  259.1 9.8 %all-to-all-start.7 = ((bf16[32,64,256]{2,1,0:T(8,128)(2,1)}), bf16[32,64,256]{2,1,0:T(8,128)(2,1)}, u32[]{:S(2)}, u32[]{:S(2)}) async-start(bf16[32,64,256]{2,1,0:T(8,128)(2,1)} %bitcast.24), calls=%async_computation.7 | async-start | bytes 2097152 | tf_op jit(solution)/shard_map/all_to_all | solution.py:107
  269.7 12.4 %scatter_custom_fusion.6 = f32[1024,256]{1,0:T(8,128)S(1)} fusion(s32[2048]{0:T(1024)S(1)} %reshape.284, f32[256,16,256]{2,1,0:T(8,128)} %bitcast_add_fusion.1, f32[]{:T(128)} %constant.13.clone.1), kind=kCustom, calls=%fused_computation.21 | custom fusion | flops 524288 | bytes 3146240 | tf_op jit(solution)/shard_map/scatter-add | solution.py:99
  282.1 13.1 %scatter_custom_fusion.7 = f32[1024,256]{1,0:T(8,128)} fusion(s32[2048]{0:T(1024)S(1)} %reshape.292, f32[256,16,256]{2,1,0:T(8,128)} %bitcast_add_fusion, f32[]{:T(128)} %constant.13.clone.1), kind=kCustom, calls=%fused_computation.19 | custom fusion | flops 524288 | bytes 3146240 | tf_op jit(solution)/shard_map/scatter-add | solution.py:99
  295.2 2.3 add.150
  302.0 11.3 %scatter_custom_fusion.1 = f32[2048]{0:T(1024)S(1)} fusion(s32[2048]{0:T(1024)S(1)} %reshape.244, f32[2048]{0:T(1024)S(1)} %reshape.246, f32[]{:T(128)} %constant.13.clone.1), kind=kCustom, calls=%fused_computation.87 | custom fusion | flops 2048 | bytes 8196 | tf_op jit(solution)/shard_map/scatter-add | solution.py:118
  313.3 11.3 %scatter_custom_fusion = f32[2048]{0:T(1024)S(1)} fusion(s32[2048]{0:T(1024)S(1)} %reshape.236, f32[2048]{0:T(1024)S(1)} %reshape.238, f32[]{:T(128)} %constant.13.clone.1), kind=kCustom, calls=%fused_computation.89 | custom fusion | flops 2048 | bytes 8196 | tf_op jit(solution)/shard_map/scatter-add | solution.py:118
  324.6 123.2 %all-reduce.6.cloned.1.call-done = f32[1024,256]{1,0:T(8,128)} async-done(((f32[1024,256]{1,0:T(8,128)}), f32[1024,256]{1,0:T(8,128)}) %all-reduce.6.cloned.1.call-update) | async-done | bytes 1048592 | tf_op jit(solution)/shard_map/psum | solution.py:128
  447.9 12.4 %psum.28 = bf16[2048]{0:T(1024)(128)(2,1)S(1)} all-reduce(bf16[2048]{0:T(1024)(128)(2,1)S(1)} %add_convert_fusion.1), channel_id=1, replica_groups=mesh['shard'=32,'dp'=8] {'dp'}, use_global_device_ids=true, to_apply=%region_2.0 | all-reduce | flops 2048 | bytes 8192 | tf_op jit(solution)/shard_map/psum | solution.py:123
  460.4 56.2 %all-reduce.8.cloned.1.call-done = f32[1024,256]{1,0:T(8,128)} async-done(((f32[1024,256]{1,0:T(8,128)}), f32[1024,256]{1,0:T(8,128)}) %all-reduce.8.cloned.1.call-update) | async-done | bytes 1048592 | tf_op jit(solution)/shard_map/psum | solution.py:128
  518.0 12.6 %scatter_custom_fusion.3 = f32[2048,256]{1,0:T(8,128)} fusion(s32[2048]{0:T(1024)S(1)} %reshape.236, bf16[2048,256]{1,0:T(8,128)(2,1)} %bitcast.28, f32[]{:T(128)} %constant.13.clone.1), kind=kCustom, calls=%fused_computation.30 | custom fusion | flops 1048576 | bytes 3145732 | tf_op jit(solution)/shard_map/scatter-add | solution.py:112
  530.6 12.3 %scatter_custom_fusion.5 = f32[2048,256]{1,0:T(8,128)} fusion(s32[2048]{0:T(1024)S(1)} %reshape.244, bf16[2048,256]{1,0:T(8,128)(2,1)} %bitcast.29, f32[]{:T(128)} %constant.13.clone.1), kind=kCustom, calls=%fused_computation.28 | custom fusion | flops 1048576 | bytes 3145732 | tf_op jit(solution)/shard_map/scatter-add | solution.py:112
  542.9 3.5 add_convert_fusion
  548.2 65.4 %all-reduce.4.cloned.1.call-done = bf16[2048,256]{1,0:T(8,128)(2,1)} async-done(((bf16[2048,256]{1,0:T(8,128)(2,1)}), bf16[2048,256]{1,0:T(8,128)(2,1)}) %all-reduce.4.cloned.1.call-update) | async-done | bytes 1048592 | tf_op jit(solution)/shard_map/psum | solution.py:122
  613.7 1.9 multiply_reduce_fusion
  616.2 2.2 abs_reduce_fusion
  (133 shorter events, 35.5 us)
Async XLA Ops:
  7.2 167.3 %copy-start = (bf16[256,512]{1,0:T(8,128)(2,1)S(1)}, bf16[256,512]{1,0:T(8,128)(2,1)}, u32[]{:S(2)}) copy-start(bf16[256,512]{1,0:T(8,128)(2,1)} %param.20) | copy-start | bytes 786436
  28.6 14.9 %copy-start.12 = (s32[32,1,64]{2,1,0:T(1,128)}, s32[32,1,64]{2,1,0:T(1,128)S(1)}, u32[]{:S(2)}) copy-start(s32[32,1,64]{2,1,0:T(1,128)S(1)} %all_to_all.62) | copy-start | bytes 24580
  28.6 14.9 %all-to-all-start = ((s32[32,1,64]{2,1,0:T(1,128)}), s32[32,1,64]{2,1,0:T(1,128)S(1)}, u32[]{:S(2)}, u32[]{:S(2)}) async-start(s32[32,1,64]{2,1,0:T(1,128)} %bitcast), calls=%async_computation | async-start | bytes 32768 | tf_op jit(solution)/shard_map/all_to_all | solution.py:82
  43.5 10.1 %copy-start.2 = (bf16[2048,256]{1,0:T(8,128)(2,1)S(1)}, bf16[2048,256]{1,0:T(8,128)(2,1)}, u32[]{:S(2)}) copy-start(bf16[2048,256]{1,0:T(8,128)(2,1)} %param.14) | copy-start | bytes 3145732
  43.5 36.4 %all-to-all-start.6 = ((bf16[32,64,256]{2,1,0:T(8,128)(2,1)}), bf16[32,64,256]{2,1,0:T(8,128)(2,1)S(1)}, u32[]{:S(2)}, u32[]{:S(2)}) async-start(bf16[32,64,256]{2,1,0:T(8,128)(2,1)} %bitcast.16), calls=%async_computation.6 | async-start | bytes 2097152 | tf_op jit(solution)/shard_map/all_to_all | solution.py:83
  62.7 22.8 %copy-start.27 = (s32[2,32]{1,0:T(2,128)S(1)}, s32[2,32]{1,0:T(2,128)}, u32[]{:S(2)}) copy-start(s32[2,32]{1,0:T(2,128)} %param.27) | copy-start | bytes 772
  62.7 24.2 %copy-start.21 = (s32[512,8]{0,1:T(8,128)S(1)}, s32[512,8]{0,1:T(8,128)}, u32[]{:S(2)}) copy-start(s32[512,8]{0,1:T(8,128)} %param.25) | copy-start | bytes 49156
  62.7 34.5 %copy-start.1 = (f32[1024,256]{1,0:T(8,128)S(1)}, f32[1024,256]{1,0:T(8,128)}, u32[]{:S(2)}) copy-start(f32[1024,256]{1,0:T(8,128)} %param.17) | copy-start | bytes 3145732
  79.9 49.2 %all-to-all-start.4 = ((bf16[32,64,256]{2,1,0:T(8,128)(2,1)}), bf16[32,64,256]{2,1,0:T(8,128)(2,1)}, u32[]{:S(2)}, u32[]{:S(2)}) async-start(bf16[32,64,256]{2,1,0:T(8,128)(2,1)} %bitcast.103), calls=%async_computation.4 | async-start | bytes 2097152 | tf_op jit(solution)/shard_map/all_to_all | solution.py:83
  97.2 8.4 %copy-start.18 = (s32[2048]{0:T(1024)S(1)}, s32[2048]{0:T(1024)}, u32[]{:S(2)}) copy-start(s32[2048]{0:T(1024)} %reshape.204) | copy-start | bytes 24580
  105.7 8.5 %copy-start.16 = (s32[2048]{0:T(1024)S(1)}, s32[2048]{0:T(1024)}, u32[]{:S(2)}) copy-start(s32[2048]{0:T(1024)} %reshape.196) | copy-start | bytes 24580
  105.7 8.5 %copy-start.17 = (s32[2048]{0:T(1024)S(1)}, s32[2048]{0:T(1024)}, u32[]{:S(2)}) copy-start(s32[2048]{0:T(1024)} %reshape.220) | copy-start | bytes 24580
  123.2 4.4 copy-start.4
  123.2 4.4 copy-start.5
  129.1 58.8 %all-to-all-start.3 = ((s32[32,1,1]{2,1,0:T(1,128)}), s32[32,1,1]{2,1,0:T(1,128)}, u32[]{:S(2)}, u32[]{:S(2)}) async-start(s32[32,1,1]{2,1,0:T(1,128)} %copy.67), calls=%async_computation.3 | async-start | bytes 32768 | tf_op jit(solution)/shard_map/all_to_all | solution.py:110
  149.5 4.3 copy-start.7
  149.5 4.3 copy-start.8
  167.6 2.8 copy-start.3
  173.2 1.3 copy-start.24
  173.2 1.5 copy-start.25
  174.8 0.7 copy-start.26
  187.9 32.0 %all-to-all-start.1 = ((s32[32,1,1]{2,1,0:T(1,128)}), s32[32,1,1]{2,1,0:T(1,128)S(1)}, u32[]{:S(2)}, u32[]{:S(2)}) async-start(s32[32,1,1]{2,1,0:T(1,128)} %copy.66), calls=%async_computation.1 | async-start | bytes 32768 | tf_op jit(solution)/shard_map/all_to_all | solution.py:110
  219.9 9.8 %copy-start.14 = (s32[32,1,1]{2,1,0:T(1,128)}, s32[32,1,1]{2,1,0:T(1,128)S(1)}, u32[]{:S(2)}) copy-start(s32[32,1,1]{2,1,0:T(1,128)S(1)} %all-to-all-done.1) | copy-start | bytes 388
  219.9 39.2 %all-to-all-start.5 = ((bf16[32,64,256]{2,1,0:T(8,128)(2,1)}), bf16[32,64,256]{2,1,0:T(8,128)(2,1)}, u32[]{:S(2)}, u32[]{:S(2)}) async-start(bf16[32,64,256]{2,1,0:T(8,128)(2,1)} %bitcast.104), calls=%async_computation.5 | async-start | bytes 2097152 | tf_op jit(solution)/shard_map/all_to_all | solution.py:107
  238.1 1.8 copy-start.6
  238.1 1.8 copy-start.10
  256.4 12.8 %copy-start.20 = (s32[256,8]{0,1:T(8,128)S(1)}, s32[256,8]{0,1:T(8,128)}, u32[]{:S(2)}) copy-start(s32[256,8]{0,1:T(8,128)} %get-tuple-element.14) | copy-start | bytes 24580
  256.4 13.1 %copy-start.19 = (s32[256,8]{0,1:T(8,128)S(1)}, s32[256,8]{0,1:T(8,128)}, u32[]{:S(2)}) copy-start(s32[256,8]{0,1:T(8,128)} %get-tuple-element.17) | copy-start | bytes 24580
  259.1 271.5 %all-to-all-start.7 = ((bf16[32,64,256]{2,1,0:T(8,128)(2,1)}), bf16[32,64,256]{2,1,0:T(8,128)(2,1)}, u32[]{:S(2)}, u32[]{:S(2)}) async-start(bf16[32,64,256]{2,1,0:T(8,128)(2,1)} %bitcast.24), calls=%async_computation.7 | async-start | bytes 2097152 | tf_op jit(solution)/shard_map/all_to_all | solution.py:107
  269.0 178.9 %all-reduce.6.cloned.1.call-start = ((), (), s32[]{:S(2)}) async-start(), calls=%async_computation.9 | async-start | bytes 2097152 | tf_op jit(solution)/shard_map/psum | solution.py:128
  295.2 4.0 copy-start.15
  295.2 5.3 copy-start.13
  297.6 218.9 %all-reduce.8.cloned.1.call-start = ((), (), s32[]{:S(2)}) async-start(), calls=%async_computation.10 | async-start | bytes 2097152 | tf_op jit(solution)/shard_map/psum | solution.py:128
  447.8 165.8 %all-reduce.4.cloned.1.call-start = ((), (), s32[]{:S(2)}) async-start(), calls=%async_computation.8 | async-start | bytes 2097152 | tf_op jit(solution)/shard_map/psum | solution.py:122
  542.9 3.5 copy-start.23
  542.9 4.1 copy-start.9
  547.0 68.5 %copy-start.22 = (f32[2048]{0:T(1024)S(1)}, f32[2048]{0:T(1024)}, u32[]{:S(2)}) copy-start(f32[2048]{0:T(1024)} %param.15) | copy-start | bytes 24580
  616.2 2.2 copy-start.11
Sparse Core Ops, SparseCore 0:
  297.7 150.0 all-reduce.5
  450.2 66.3 all-reduce.7
  546.5 67.0 all-reduce.3
